TPU v7x, 256 devices: a whole 4x4x8 slice. The times are simulated.
256 devices in a mesh: frame: 64 (over y, x_lo, z), patch: 4 (over x_hi, core).
Axes of the slice: x: 4 (x_hi: 2, x_lo: 2; x = x_hi * 2 + x_lo), y: 4, z: 8, core: 2. Of those that a mesh axis runs over, the one named last changes fastest.
Arguments:
- sky_image: float32 [64, 512, 1024], P('frame', None, 'patch'), may hold values from 0.5 to 1.5
- coefficients: float32 [64, 32, 64], P('frame', 'patch'), may hold values from -0.9 to 0.9
- mode_basis: float32 [64, 20736], replicated, may hold values from -6 to 6
- aperture: int32 [144, 144], replicated, may hold values from 0 to 1, as said below
Outputs:
- mode_gradient: float32 [64, 32, 64], P('frame', 'patch')
- object_spectrum: float32 [32, 2, 20736], P('patch', None, 'frame')
Inputs may be any that keep to these rules, and one draw needn't show every extreme that they name: `aperture`: 0 outside an annulus centred at (72, 72) with outer radius between 28 and 36 pixels and a central obstruction; inside it, each pixel is 1 except for randomly placed dead pixels, which are 0.
All inputs are finite; a program needn't handle non-finite values.
Results may differ from a plain program's by a relative error of at most 0.0003.
Values sent between devices are 32-bit elements; how exact they have to be, the bound alone decides.
A program may use at most 128 MiB of HBM per device.

v0:
```python
import math
import jax
import jax.numpy as jnp
from jax import lax
from jax.sharding import PartitionSpec as P

P_SIZE = 144
RIM = 8
reg_weight = 0.02
highest = lax.Precision.HIGHEST


def padded_2(array, sides, width):
    for axis, dim in sides:
        size, length = (lax.axis_size(axis), array.shape[dim])
        up = [(i, (i + 1) % size) for i in range(size - 1)]
        down = [(j, i) for i, j in up]
        last = lax.slice_in_dim(array, length - width, length, axis=dim)
        initial = lax.slice_in_dim(array, 0, width, axis=dim)
        before = lax.ppermute(last, axis, up)
        after = lax.ppermute(initial, axis, down)
        array = jnp.concatenate([before, array, after], axis=dim)
    return array


def window_table():
    offsets = jnp.arange(P_SIZE, dtype=jnp.float32)
    distance = jnp.minimum(offsets, P_SIZE - 1 - offsets)
    taper_value = 0.3 + 0.7 * jnp.sin(math.pi * (distance + 1.0) / (2.0 * (RIM + 1))) ** 2
    profile = jnp.where(distance < RIM, taper_value, 1.0)
    return profile[:, None] * profile[None, :]


def fourier_tables():
    position = jnp.arange(P_SIZE, dtype=jnp.int32)
    product = position[:, None] * position[None, :] % P_SIZE
    angles = 2.0 * math.pi / P_SIZE * product.astype(jnp.float32)
    return (jnp.cos(angles), jnp.sin(angles))


def left_mult(table, field_stack):
    return jnp.einsum("ab,fpbc->fpac", table, field_stack, precision=highest)


def right_mult(field_stack, table):
    return jnp.einsum("fpab,bc->fpac", field_stack, table, precision=highest)


def transform(real_part, imag_part, tables):
    cosine_table, sine_table = tables
    if imag_part is None:
        left_real = left_mult(cosine_table, real_part)
        left_imag = -left_mult(sine_table, real_part)
    else:
        left_real = left_mult(cosine_table, real_part) + left_mult(sine_table, imag_part)
        left_imag = left_mult(cosine_table, imag_part) - left_mult(sine_table, real_part)
    out_real = right_mult(left_real, cosine_table) + right_mult(left_imag, sine_table)
    out_imag = right_mult(left_imag, cosine_table) - right_mult(left_real, sine_table)
    return (out_real, out_imag)


def body(sky_image, coefficients, mode_basis, aperture):
    frames_here, row_total, column_total = sky_image.shape
    patches_here = coefficients.shape[1]
    tile_side = P_SIZE - 2 * RIM
    tables = fourier_tables()
    window = window_table()
    widened = padded_2(sky_image, (("patch", 2),), RIM)
    padded = jnp.pad(widened, ((0, 0), (RIM, RIM), (0, 0)))
    row_count = row_total // tile_side
    column_count = column_total // tile_side
    blocks = []
    for column_place in range(column_count):
        for row_place in range(row_count):
            blocks.append(
                padded[
                    :,
                    row_place * tile_side : row_place * tile_side + P_SIZE,
                    column_place * tile_side : column_place * tile_side + P_SIZE,
                ]
            )
    patches = jnp.stack(blocks, axis=1)
    data_real, data_imag = transform(window * patches, None, tables)
    data_real = data_real / P_SIZE
    data_imag = data_imag / P_SIZE
    pupil_mask = aperture.astype(jnp.float32)
    pupil_area = jnp.sum(pupil_mask)

    def transfer_map(mode_weights):
        phase_map = jnp.einsum("fpk,kx->fpx", mode_weights, mode_basis, precision=highest).reshape(
            frames_here, patches_here, P_SIZE, P_SIZE
        )
        focal_real, focal_imag = transform(
            pupil_mask * jnp.cos(phase_map), pupil_mask * jnp.sin(phase_map), tables
        )
        intensity = (focal_real**2 + focal_imag**2) / (P_SIZE * P_SIZE * pupil_area)
        return transform(intensity, None, tables)

    (otf_real, otf_imag), pullback = jax.vjp(transfer_map, coefficients)
    numer_real = jnp.sum(otf_real * data_real + otf_imag * data_imag, axis=0)
    numer_imag = jnp.sum(otf_real * data_imag - otf_imag * data_real, axis=0)
    power = jnp.sum(otf_real**2 + otf_imag**2, axis=0)
    spectra = jnp.stack([numer_real, numer_imag, power], axis=1).reshape(
        patches_here, 3, P_SIZE * P_SIZE
    )
    frame_total = frames_here * lax.axis_size("frame")
    damping = reg_weight * frame_total
    share = P_SIZE * P_SIZE // lax.axis_size("frame")
    totals = lax.psum(spectra, "frame")
    denominator = totals[:, 2] + damping
    estimate = totals[:, 0:2] / denominator[:, None]
    own_part = lax.dynamic_slice_in_dim(estimate, lax.axis_index("frame") * share, share, 2)
    object_real = estimate[:, 0].reshape(patches_here, P_SIZE, P_SIZE)[None]
    object_imag = estimate[:, 1].reshape(patches_here, P_SIZE, P_SIZE)[None]
    error_real = data_real - (object_real * otf_real - object_imag * otf_imag)
    error_imag = data_imag - (object_real * otf_imag + object_imag * otf_real)
    scale_factor = 2.0 / (P_SIZE * P_SIZE)
    cotangent_real = -scale_factor * (error_real * object_real + error_imag * object_imag)
    cotangent_imag = scale_factor * (error_real * object_imag - error_imag * object_real)
    gradient = pullback((cotangent_real, cotangent_imag))[0]
    mode_total = lax.psum(jnp.sum(gradient, axis=0), "frame")
    mode_gradient = gradient - mode_total[None] / frame_total
    return (mode_gradient, own_part)


def solution(mesh):
    in_specs = (P("frame", None, "patch"), P("frame", "patch", None), P(), P())
    out_specs = (P("frame", "patch", None), P("patch", None, "frame"))
    return jax.shard_map(body, mesh=mesh, in_specs=in_specs, out_specs=out_specs, check_vma=False)
```

profile of v0, /device:TPU:4, one launch (start us, length us, event | category | flops | bytes accessed | tf_op | source)
XLA Modules:
  0.0 938.4 jit_solution(11270163691090871212)
XLA Ops:
  7.2 2.0 fusion.346
  9.2 1.9 collective-permute-start
  11.1 5.1 collective-permute-start.1
  16.3 0.9 convert_element_type.74
  18.0 6.6 fusion.345
  24.6 0.8 copy-done.9
  25.4 0.9 cos.58
  26.9 1.9 sin.70
  28.8 1.8 copy.45
  30.7 1.7 fusion.38
  32.3 1.7 fusion.34
  34.0 1.7 fusion.18
  35.7 3.2 fusion.89
  38.9 2.1 fusion.17
  41.0 3.2 fusion.86
  44.2 3.2 convolution_add_fusion.8
  47.4 3.2 convolution_subtract_fusion.2
  51.2 3.3 fusion
  54.5 3.4 convolution_bitcast_fusion
  58.0 3.2 fusion.83
  61.2 3.2 fusion.81
  64.4 3.2 convolution_add_fusion.7
  67.7 1.3 select_maximum_fusion
  69.3 1.0 constant_dynamic-update-slice_fusion
  70.7 3.2 convolution_bitcast_fusion.1
  73.9 3.2 fusion.1
  77.2 3.2 fusion.92
  80.3 3.2 fusion.79
  83.5 3.6 fusion.19
  87.1 3.2 fusion.16
  90.3 5.7 multiply_add_fusion.1
  96.0 2.7 stack.11
  98.7 2.7 stack.12
  101.4 2.7 stack.26
  104.1 2.9 pad_maximum_fusion
  107.0 3.0 cos.59
  110.0 3.1 sin.71
  113.2 3.0 copy.63
  116.1 2.9 copy.66
  119.0 597.5 %all-reduce.3.cloned.1.call-done = f32[8,3,20736]{2,0,1:T(8,128)} async-done(((f32[8,3,20736]{2,0,1:T(8,128)}), f32[8,3,20736]{2,0,1:T(8,128)}) %all-reduce.3.cloned.1.call-update) | async-done | bytes 1990672 | tf_op jit(solution)/shard_map/psum | solution.py:109
  716.6 1.1 fusion.43
  717.7 1.4 slice_divide_fusion
  719.2 1.3 fusion.344
  720.7 3.0 broadcast_in_dim_reshape_squeeze.6
  723.6 3.0 broadcast_in_dim_reshape_squeeze.7
  726.6 3.3 add_multiply_fusion
  729.9 1.7 fusion.32
  731.6 1.7 fusion.77
  733.3 1.7 fusion.13
  734.9 1.7 fusion.15
  736.6 3.4 fusion.58
  740.0 3.2 fusion.12
  743.8 1.7 fusion.24
  745.5 1.7 fusion.28
  747.2 1.7 convolution_add_fusion.3
  748.9 3.6 fusion.22
  752.5 3.2 fusion.20
  755.6 1.7 fusion.10
  757.3 3.1 fusion.9
  760.5 3.2 fusion.6
  764.3 0.7 reshape.377
  765.1 6.1 fusion.347
  771.2 158.1 %psum.15 = f32[8,64]{1,0:T(8,128)S(1)} all-reduce(f32[8,64]{1,0:T(8,128)S(1)} %fusion.347), channel_id=1, replica_groups=mesh['frame'=64,'patch'=4] {'frame'}, use_global_device_ids=true, to_apply=%region_2.3 | all-reduce | flops 512 | bytes 4096 | tf_op jit(solution)/shard_map/psum | solution.py:121
  929.9 0.8 constant_dynamic-slice_fusion
  (49 shorter events, 4.9 us)
Async XLA Ops:
  7.2 10.8 %copy-start = (f32[1,8,64]{2,1,0:T(8,128)S(1)}, f32[1,8,64]{2,1,0:T(8,128)}, u32[]{:S(2)}) copy-start(f32[1,8,64]{2,1,0:T(8,128)} %param.5) | copy-start | bytes 6148
  7.2 10.0 %copy-start.13 = (s32[144,144]{1,0:T(8,128)S(1)}, s32[144,144]{1,0:T(8,128)}, u32[]{:S(2)}) copy-start(s32[144,144]{1,0:T(8,128)} %param.7) | copy-start | bytes 248836
  7.2 709.4 %all-reduce.3.cloned.1.call-start = ((), (), s32[]{:S(2)}) async-start(), calls=%async_computation | async-start | bytes 3981312 | tf_op jit(solution)/shard_map/psum | solution.py:109
  9.2 58.5 %collective-permute-start = (f32[1,512,8]{2,1,0:T(8,128)}, f32[1,512,8]{2,1,0:T(8,128)S(1)}, u32[]{:S(2)}, u32[]{:S(2)}) collective-permute-start(f32[1,512,8]{2,1,0:T(8,128)} %get-tuple-element.13), channel_id=1, source_target_pairs={{0,1},{1,2},{2,3},{4,5},{5,6},{6,7},{8,9},{9,10},{10,11},{12,13},{... | collective-permute-start | bytes 49160 | tf_op jit(solution)/shard_map/ppermute | solution.py:20
  11.1 56.6 %collective-permute-start.1 = (f32[1,512,8]{2,1,0:T(8,128)}, f32[1,512,8]{2,1,0:T(8,128)}, u32[]{:S(2)}, u32[]{:S(2)}) collective-permute-start(f32[1,512,8]{2,1,0:T(8,128)} %get-tuple-element.14), channel_id=1, source_target_pairs={{1,0},{2,1},{3,2},{5,4},{6,5},{7,6},{9,8},{10,9},{11,10},{13,12},{... | collective-permute-start | bytes 49160 | tf_op jit(solution)/shard_map/ppermute | solution.py:21
  18.0 20.9 %copy-start.6 = (f32[144,144]{0,1:T(8,128)}, f32[144,144]{0,1:T(8,128)S(1)}, u32[]{:S(2)}) copy-start(f32[144,144]{0,1:T(8,128)S(1)} %copy.38) | copy-start | bytes 248836
  24.6 0.9 copy-start.9
  24.6 2.3 copy-start.8
  47.4 7.1 copy-start.4
  64.4 3.3 copy-start.2
  90.3 5.7 copy-start.3
  719.1 1.5 copy-start.10
  745.5 1.7 copy-start.5
  755.6 1.7 copy-start.7
  755.6 1.7 copy-start.12
  757.3 3.2 copy-start.11
  765.1 166.3 %copy-start.1 = (f32[1,8,64]{2,1,0:T(8,128)S(1)}, f32[1,8,64]{2,1,0:T(8,128)}, u32[]{:S(2)}) copy-start(f32[1,8,64]{2,1,0:T(8,128)} %param.5) | copy-start | bytes 6148
Sparse Core Ops, SparseCore 0:
  107.2 609.3 all-reduce.2
where the time goes:
time: 949 us; the launch traced here: 938 us
  waiting for transfers between devices  598 us (63%)
  blocking collectives  158 us (17%)
  matrix products  107 us (11%)
  local copies, waits for them, and re-layouts  40.5 us (4%)
  between operations  15.4 us (2%)
  other arithmetic  12.6 us (1%)
    psum x1, waiting for transfers between devices, body(): totals = lax.psum(spectra, 'frame')  598 us
    psum x1, blocking collectives, body(): mode_total = lax.psum(jnp.sum(gradient, axis=0), 'frame')  158 us
    dot_general x20, matrix products, right_mult(): return jnp.einsum('fpab,bc->fpac', field_stack, table, precision=highest)  54.5 us
    dot_general x14, matrix products, left_mult(): return jnp.einsum('ab,fpbc->fpac', table, field_stack, precision=highest)  40 us
  transfers between devices with their start and end apart: 3, of which 1 were waited for; matrix products, arithmetic and copies ran while one was open for 7% of the time, Pallas kernels for 0%

commit v1 on v0

--- a/solution.py
+++ b/solution.py
@@ -118,7 +118,9 @@
     cotangent_real = -scale_factor * (error_real * object_real + error_imag * object_imag)
     cotangent_imag = scale_factor * (error_real * object_imag - error_imag * object_real)
     gradient = pullback((cotangent_real, cotangent_imag))[0]
-    mode_total = lax.psum(jnp.sum(gradient, axis=0), "frame")
+    x = jnp.sum(gradient, axis=0)
+    pieces = lax.all_gather(x, "frame")
+    mode_total = jnp.sum(pieces, axis=0)
     mode_gradient = gradient - mode_total[None] / frame_total
     return (mode_gradient, own_part)
 

time: 949 us -> 948 us (level)
    psum x1 -> x0, blocking collectives: 158 us -> none  [body(): mode_total = lax.psum(jnp.sum(gradient, axis=0), 'frame')]
    all_gather x0 -> x1, blocking collectives: none -> 157 us  [body(): pieces = lax.all_gather(x, 'frame')]
where the time goes in v1:
time: 948 us; the launch traced here: 938 us
  waiting for transfers between devices  597 us (63%)
  blocking collectives  157 us (17%)
  matrix products  106 us (11%)
  local copies, waits for them, and re-layouts  40.3 us (4%)
  between operations  15.4 us (2%)
  other arithmetic  14.5 us (2%)
    psum x1, waiting for transfers between devices, body(): totals = lax.psum(spectra, 'frame')  597 us
    all_gather x1, blocking collectives, body(): pieces = lax.all_gather(x, 'frame')  157 us
    dot_general x20, matrix products, right_mult(): return jnp.einsum('fpab,bc->fpac', field_stack, table, precision=highest)  53.8 us
    dot_general x14, matrix products, left_mult(): return jnp.einsum('ab,fpbc->fpac', table, field_stack, precision=highest)  39.9 us
  transfers between devices with their start and end apart: 3, of which 1 were waited for; matrix products, arithmetic and copies ran while one was open for 7% of the time, Pallas kernels for 0%

profile of v1, /device:TPU:4, one launch (start us, length us, event | category | flops | bytes accessed | tf_op | source)
XLA Modules:
  0.0 937.5 jit_solution(2380939509024498990)
XLA Ops:
  7.2 2.0 fusion.346
  9.2 1.9 collective-permute-start
  11.1 5.1 collective-permute-start.1
  16.3 0.9 convert_element_type.74
  18.0 6.6 fusion.345
  24.6 0.8 copy-done.9
  25.4 0.9 cos.58
  26.9 1.9 sin.70
  28.8 1.8 copy.45
  30.7 1.7 fusion.38
  32.3 1.7 fusion.34
  34.0 1.7 fusion.18
  35.7 3.1 fusion.89
  38.8 2.1 fusion.17
  40.9 3.1 fusion.86
  44.1 3.1 convolution_add_fusion.8
  47.2 3.1 convolution_subtract_fusion.2
  51.0 3.2 fusion
  54.2 3.4 convolution_bitcast_fusion
  57.7 3.2 fusion.83
  60.9 3.2 fusion.81
  64.1 3.1 convolution_add_fusion.7
  67.3 1.6 select_maximum_fusion
  68.9 1.0 maximum_dynamic-update-slice_fusion
  69.9 1.0 fusion.52
  71.0 1.0 constant_dynamic-update-slice_fusion
  72.2 3.2 convolution_bitcast_fusion.1
  75.4 3.2 fusion.1
  78.6 3.1 fusion.92
  81.7 3.5 fusion.79
  85.2 3.1 fusion.19
  88.3 3.2 fusion.16
  91.5 5.6 multiply_add_fusion.1
  97.1 2.7 stack.11
  99.9 2.7 stack.12
  102.6 2.7 stack.26
  105.2 2.9 pad_maximum_fusion
  108.2 3.0 cos.59
  111.2 3.1 sin.71
  114.3 3.0 copy.63
  117.3 2.9 copy.66
  120.2 596.9 %all-reduce.3.cloned.1.call-done = f32[8,3,20736]{2,0,1:T(8,128)} async-done(((f32[8,3,20736]{2,0,1:T(8,128)}), f32[8,3,20736]{2,0,1:T(8,128)}) %all-reduce.3.cloned.1.call-update) | async-done | bytes 1990672 | tf_op jit(solution)/shard_map/psum | solution.py:109
  717.1 1.1 fusion.43
  718.2 1.5 slice_divide_fusion
  719.7 1.3 fusion.344
  721.2 3.0 broadcast_in_dim_reshape_squeeze.6
  724.2 3.0 broadcast_in_dim_reshape_squeeze.7
  727.2 3.0 add_multiply_fusion
  730.2 1.7 fusion.32
  731.9 1.7 fusion.77
  733.5 1.7 fusion.13
  735.2 1.7 fusion.15
  736.9 3.3 fusion.58
  740.2 3.1 fusion.12
  743.9 1.7 fusion.24
  745.6 1.7 fusion.28
  747.3 1.7 convolution_add_fusion.3
  749.0 3.6 fusion.22
  752.6 3.2 fusion.20
  755.8 1.7 fusion.10
  757.5 3.2 fusion.9
  760.7 3.3 fusion.6
  765.3 6.1 fusion.347
  771.4 156.9 %all-gather = f32[512,64]{1,0:T(8,128)S(1)} all-gather(f32[8,64]{1,0:T(8,128)S(1)} %fusion.347), channel_id=2, replica_groups=mesh['frame'=64,'patch'=4] {'frame'}, dimensions={0}, use_global_device_ids=true | all-gather | bytes 133120 | tf_op jit(solution)/shard_map/all_gather | solution.py:122
  (50 shorter events, 6.1 us)
Async XLA Ops:
  7.2 10.8 %copy-start = (f32[1,8,64]{2,1,0:T(8,128)S(1)}, f32[1,8,64]{2,1,0:T(8,128)}, u32[]{:S(2)}) copy-start(f32[1,8,64]{2,1,0:T(8,128)} %param.5) | copy-start | bytes 6148
  7.2 10.0 %copy-start.13 = (s32[144,144]{1,0:T(8,128)S(1)}, s32[144,144]{1,0:T(8,128)}, u32[]{:S(2)}) copy-start(s32[144,144]{1,0:T(8,128)} %param.7) | copy-start | bytes 248836
  7.2 709.9 %all-reduce.3.cloned.1.call-start = ((), (), s32[]{:S(2)}) async-start(), calls=%async_computation | async-start | bytes 3981312 | tf_op jit(solution)/shard_map/psum | solution.py:109
  9.2 58.1 %collective-permute-start = (f32[1,512,8]{2,1,0:T(8,128)}, f32[1,512,8]{2,1,0:T(8,128)}, u32[]{:S(2)}, u32[]{:S(2)}) collective-permute-start(f32[1,512,8]{2,1,0:T(8,128)} %get-tuple-element.13), channel_id=1, source_target_pairs={{0,1},{1,2},{2,3},{4,5},{5,6},{6,7},{8,9},{9,10},{10,11},{12,13},{... | collective-permute-start | bytes 49160 | tf_op jit(solution)/shard_map/ppermute | solution.py:20
  11.1 56.2 %collective-permute-start.1 = (f32[1,512,8]{2,1,0:T(8,128)}, f32[1,512,8]{2,1,0:T(8,128)}, u32[]{:S(2)}, u32[]{:S(2)}) collective-permute-start(f32[1,512,8]{2,1,0:T(8,128)} %get-tuple-element.14), channel_id=1, source_target_pairs={{1,0},{2,1},{3,2},{5,4},{6,5},{7,6},{9,8},{10,9},{11,10},{13,12},{... | collective-permute-start | bytes 49160 | tf_op jit(solution)/shard_map/ppermute | solution.py:21
  18.0 20.8 %copy-start.6 = (f32[144,144]{0,1:T(8,128)}, f32[144,144]{0,1:T(8,128)S(1)}, u32[]{:S(2)}) copy-start(f32[144,144]{0,1:T(8,128)S(1)} %copy.38) | copy-start | bytes 248836
  24.6 0.9 copy-start.9
  24.6 2.3 copy-start.8
  47.2 7.0 copy-start.4
  64.0 3.2 copy-start.2
  91.5 5.6 copy-start.3
  719.7 1.5 copy-start.10
  745.6 1.7 copy-start.5
  755.8 1.7 copy-start.7
  755.8 1.7 copy-start.12
  757.5 3.2 copy-start.11
  765.3 165.2 %copy-start.1 = (f32[1,8,64]{2,1,0:T(8,128)S(1)}, f32[1,8,64]{2,1,0:T(8,128)}, u32[]{:S(2)}) copy-start(f32[1,8,64]{2,1,0:T(8,128)} %param.5) | copy-start | bytes 6148
Sparse Core Ops, SparseCore 0:
  108.3 608.7 all-reduce.2
